TPU v7x, 128 devices: a whole 4x4x4 slice. The times are simulated.
128 devices in a mesh: dp: 32 (over x, z, core), mp: 4 (over y).
Axes of the slice: x: 4, y: 4, z: 4, core: 2. Of those that a mesh axis runs over, the one named last changes fastest.
Arguments:
- hidden_in: bfloat16 [32768, 2048], P('dp', 'mp'), may hold values from -6 to 6
- token_ids: int32 [32768], P('dp'), may hold values from 0 to 128001, as said below
- passage_counts: int32 [64], P('dp'), may hold values from 1 to 4, as said below
- positive_doc: int32 [4096], P('dp'), may hold values from 0 to 63
- queries: bfloat16 [4096, 2048], P('dp', 'mp'), may hold values from -6 to 6
- norm_gain: float32 [2048], replicated, may hold values from 0.5 to 1.5
- w_gate: bfloat16 [2048, 7168], P(None, 'mp'), may hold values from -0.125 to 0.125
- w_up: bfloat16 [2048, 7168], P(None, 'mp'), may hold values from -0.125 to 0.125
- w_down: bfloat16 [7168, 2048], P('mp'), may hold values from -0.0625 to 0.0625
Outputs:
- query_loss: float32 [4096], P('dp')
- hidden_grad: bfloat16 [32768, 2048], P('dp', 'mp')
Inputs may be any that keep to these rules, and one draw needn't show every extreme that they name: `passage_counts`: A document has 1 to 4 passages; every draw has a dp index whose documents all have 4. The live passages hold 160 passages in all. `token_ids`: 128001 marks padding; it stands only at the tail of a document's last live passage, and every live passage has a token that is not padding.
All inputs are finite; a program needn't handle non-finite values.
Results may differ from a plain program's by a relative error of at most 0.023.
Values may be sent and summed in bfloat16 or wider, within the bound.
No kernel may reach another device: no remote copies, remote signals or barrier semaphores. Data moves between devices by JAX's collectives and lax.ppermute only.
A program may use at most 128 MiB of HBM per device.

v0:
```python
import math
import jax
import jax.numpy as jnp
from jax import lax
from jax.sharding import PartitionSpec as P

L = 128
pad_token = 128001
score_scale = 20.0
loss_seed = 4096.0
norm_epsilon = 1e-05
unit_epsilon = 1e-06


def sent_to_all(x, axis):
    copies = jnp.broadcast_to(x, (lax.axis_size(axis), *x.shape))
    return lax.all_to_all(copies, axis, split_axis=0, concat_axis=0, tiled=True)


def joined_along(blocks, dim):
    lengths = list(blocks.shape[1:])
    lengths[dim] *= blocks.shape[0]
    return jnp.moveaxis(blocks, 0, dim).reshape(lengths)


def gathered_copies(x, axis, dim):
    blocks = sent_to_all(x, axis)
    return joined_along(blocks, dim)


def cut_along(x, dim, devices):
    before, after = (x.shape[:dim], x.shape[dim + 1 :])
    return jnp.moveaxis(x.reshape(*before, devices, -1, *after), dim, 0)


def summed_on_arrival(x, axis, dim):
    blocks = cut_along(x, dim, lax.axis_size(axis))
    arrived = lax.all_to_all(blocks, axis, split_axis=0, concat_axis=0, tiled=True)
    return arrived.astype(jnp.float32).sum(axis=0)


def sent_together(arrays, axis, dim, along):
    widths = [math.prod(a.shape[along:]) for a in arrays]
    both = jnp.concatenate(
        [a.reshape(*a.shape[:along], w) for a, w in zip(arrays, widths)], axis=along
    )
    result = summed_on_arrival(both, axis, dim)
    blocks = jnp.split(result, [sum(widths[:k]) for k in range(1, len(widths))], axis=along)
    return tuple(
        (b.reshape(*result.shape[:along], *a.shape[along:]) for a, b in zip(arrays, blocks))
    )


def contract_rows(left, right):
    return lax.dot_general(
        left, right, (((1,), (1,)), ((), ())), preferred_element_type=jnp.float32
    )


def packing_order(received_flag, received_mask, slot_capacity):
    flag = received_flag.reshape(-1).astype(jnp.float32)
    place = jnp.cumsum(flag) - flag
    packed_rows = flag[None, :] * (
        place[None, :] == jnp.arange(slot_capacity, dtype=jnp.float32)[:, None]
    ).astype(jnp.float32)
    packed_half_rows = packed_rows.astype(jnp.bfloat16)
    task_row_mask = jnp.dot(
        packed_half_rows,
        received_mask.reshape(flag.shape[0], -1),
        preferred_element_type=jnp.float32,
    )
    return (packed_rows, packed_half_rows, task_row_mask)


def per_device(
    hidden_in, token_ids, passage_counts, positive_doc, queries, norm_gain, w_gate, w_up, w_down
):
    dp_count = lax.axis_size("dp")
    row_count, part_width = hidden_in.shape
    model_width = norm_gain.shape[0]
    docs_here = passage_counts.shape[0]
    quarters = 4
    block_len = L // quarters
    src_blocks = row_count // block_len
    most_pass = src_blocks // (docs_here * quarters)
    slot_count = src_blocks // dp_count
    slot_capacity = docs_here * 2 * (most_pass + 1)
    passes_here = docs_here * most_pass
    received = dp_count * slot_count
    all_counts = lax.all_gather(passage_counts, "dp", axis=0, tiled=True)
    doc_total = all_counts.shape[0]
    before = (jnp.arange(doc_total, dtype=jnp.int32) < lax.axis_index("dp") * docs_here).astype(
        jnp.int32
    )
    offset = quarters * jnp.sum(all_counts * before)
    block_index = jnp.arange(src_blocks, dtype=jnp.int32)
    live_block = block_index // quarters % most_pass < jnp.repeat(
        passage_counts, most_pass * quarters
    )
    live_int = live_block.astype(jnp.int32)
    global_order = offset + jnp.cumsum(live_int) - live_int
    target = global_order % dp_count
    token_live = (token_ids.reshape(src_blocks, block_len) != pad_token) & live_block[:, None]
    device_hit = live_block.astype(jnp.float32)[:, None] * (
        target[:, None] == jnp.arange(dp_count, dtype=jnp.int32)[None, :]
    ).astype(jnp.float32)
    earlier = jnp.cumsum(device_hit, axis=0) - device_hit
    slot_match = (
        earlier[:, :, None] == jnp.arange(slot_count, dtype=jnp.float32)[None, None, :]
    ).astype(jnp.float32)
    select = (device_hit[:, :, None] * slot_match).reshape(src_blocks, received).T
    select_half = select.astype(jnp.bfloat16)
    send_mask = jnp.dot(
        select_half, token_live.astype(jnp.bfloat16), preferred_element_type=jnp.float32
    )
    send_mask = send_mask.astype(jnp.bfloat16).reshape(dp_count, slot_count, block_len)
    send_flag = jnp.sum(select, axis=1).astype(jnp.bfloat16).reshape(dp_count, slot_count)
    mp_start = lax.axis_index("mp") * part_width
    send = jnp.dot(
        select_half,
        hidden_in.reshape(src_blocks, block_len * part_width),
        preferred_element_type=jnp.float32,
    )
    send = send.astype(jnp.bfloat16).reshape(dp_count, slot_count, block_len, part_width)
    got, received_mask, received_flag = (
        lax.all_to_all(send, "dp", split_axis=0, concat_axis=0, tiled=True),
        lax.all_to_all(send_mask, "dp", split_axis=0, concat_axis=0, tiled=True),
        lax.all_to_all(send_flag, "dp", split_axis=0, concat_axis=0, tiled=True),
    )
    packed_rows, packed_half_rows, task_row_mask = packing_order(
        received_flag, received_mask, slot_capacity
    )
    own_rows = jnp.dot(
        packed_half_rows,
        got.reshape(received, block_len * part_width),
        preferred_element_type=jnp.float32,
    )
    own_rows = own_rows.astype(jnp.bfloat16).reshape(slot_capacity * block_len, part_width)
    task_rows = gathered_copies(own_rows, "mp", 1)
    row_float = task_rows.astype(jnp.float32)
    rms_scale = lax.rsqrt(jnp.mean(row_float * row_float, axis=1, keepdims=True) + norm_epsilon)
    normed = (row_float * rms_scale * norm_gain[None, :]).astype(jnp.bfloat16)
    gate = jnp.dot(normed, w_gate, preferred_element_type=jnp.float32)
    up = jnp.dot(normed, w_up, preferred_element_type=jnp.float32)
    sigmoid_gate = jax.nn.sigmoid(gate)
    hidden = (gate * sigmoid_gate * up).astype(jnp.bfloat16)
    layer_part = jnp.dot(hidden, w_down, preferred_element_type=jnp.float32)
    token_weight = task_row_mask[:, :, None]
    layer_pool = jnp.sum(
        layer_part.reshape(slot_capacity, block_len, model_width) * token_weight, axis=1
    )
    layer_pool = summed_on_arrival(layer_pool.astype(jnp.bfloat16), "mp", 1)
    own_input = own_rows.astype(jnp.float32)
    pooled = (
        jnp.sum(own_input.reshape(slot_capacity, block_len, part_width) * token_weight, axis=1)
        + layer_pool
    )
    spread = jnp.dot(packed_rows.T, pooled)
    home = lax.all_to_all(
        spread.reshape(dp_count, slot_count, part_width).astype(jnp.bfloat16),
        "dp",
        split_axis=0,
        concat_axis=0,
        tiled=True,
    ).astype(jnp.float32)
    block_sums = jnp.dot(select.T, home.reshape(received, part_width))
    passage_sum = block_sums.reshape(passes_here, quarters, part_width).sum(axis=1)
    token_total = jnp.sum(
        token_live.reshape(passes_here, quarters * block_len).astype(jnp.float32), axis=1
    )
    divisor = jnp.maximum(token_total, 1.0)
    passage_vec = (passage_sum / divisor[:, None]).astype(jnp.bfloat16)
    all_vec = lax.all_gather(passage_vec, "dp", axis=0, tiled=True)
    pass_total = all_vec.shape[0]
    all_live = (
        jnp.arange(pass_total, dtype=jnp.int32) % most_pass < jnp.repeat(all_counts, most_pass)
    ).astype(jnp.float32)
    vec_float = all_vec.astype(jnp.float32)
    query_float = queries.astype(jnp.float32)
    score_part = contract_rows(queries, all_vec)
    raw_score, passage_sq, query_sq = (
        lax.psum(score_part.astype(jnp.bfloat16), "mp").astype(jnp.float32),
        lax.psum(jnp.sum(vec_float * vec_float, axis=1).astype(jnp.bfloat16), "mp").astype(
            jnp.float32
        ),
        lax.psum(jnp.sum(query_float * query_float, axis=1).astype(jnp.bfloat16), "mp").astype(
            jnp.float32
        ),
    )
    query_scale = lax.rsqrt(query_sq + unit_epsilon)
    passage_scale = lax.rsqrt(passage_sq + unit_epsilon)
    scores = score_scale * raw_score * query_scale[:, None] * passage_scale[None, :]
    weights = all_live[None, :] * jnp.exp(scores)
    doc_mass = weights.reshape(queries.shape[0], doc_total, most_pass).sum(axis=2)
    total_mass = doc_mass.sum(axis=1)
    positive_hit = (
        positive_doc[:, None] == jnp.arange(doc_total, dtype=jnp.int32)[None, :]
    ).astype(jnp.float32)
    positive_mass = jnp.sum(doc_mass * positive_hit, axis=1)
    query_loss = jnp.log(total_mass) - jnp.log(positive_mass)
    positive_pass = jnp.repeat(positive_hit, most_pass, axis=1)
    coefficient = (
        loss_seed
        * score_scale
        * query_scale[:, None]
        * (weights / total_mass[:, None] - positive_pass * weights / positive_mass[:, None])
    )
    weighted_queries = lax.dot_general(
        coefficient.astype(jnp.bfloat16),
        queries,
        (((0,), (0,)), ((), ())),
        preferred_element_type=jnp.float32,
    )
    norm_term = jnp.sum(coefficient * raw_score, axis=0)
    vec_grad, norm_grad = sent_together(
        (weighted_queries.astype(jnp.bfloat16), norm_term.astype(jnp.bfloat16)), "dp", 0, 1
    )
    own_scale = lax.dynamic_slice_in_dim(
        passage_scale, lax.axis_index("dp") * passes_here, passes_here
    )
    own_vec = passage_vec.astype(jnp.float32)
    vec_change = own_scale[:, None] * vec_grad - own_vec * (own_scale**3 * norm_grad)[:, None]
    token_grad = (vec_change / divisor[:, None]).astype(jnp.bfloat16)
    block_grad = jnp.repeat(token_grad, quarters, axis=0)
    grad_send = jnp.dot(select_half, block_grad, preferred_element_type=jnp.float32).astype(
        jnp.bfloat16
    )
    grad_got = lax.all_to_all(
        grad_send.reshape(dp_count, slot_count, part_width),
        "dp",
        split_axis=0,
        concat_axis=0,
        tiled=True,
    )
    grad_task = jnp.dot(
        packed_half_rows, grad_got.reshape(received, part_width), preferred_element_type=jnp.float32
    ).astype(jnp.bfloat16)
    grad_full = lax.all_gather(grad_task, "mp", axis=1, tiled=True)
    out_grad = (
        (token_weight * grad_full[:, None, :].astype(jnp.float32))
        .astype(jnp.bfloat16)
        .reshape(slot_capacity * block_len, model_width)
    )
    own_out_grad = (token_weight * grad_task[:, None, :].astype(jnp.float32)).reshape(
        slot_capacity * block_len, part_width
    )
    hidden_grad = contract_rows(out_grad, w_down)
    gate_grad = (hidden_grad * up * sigmoid_gate * (1.0 + gate * (1.0 - sigmoid_gate))).astype(
        jnp.bfloat16
    )
    up_grad = (hidden_grad * gate * sigmoid_gate).astype(jnp.bfloat16)
    normed_grad = contract_rows(gate_grad, w_gate) + contract_rows(up_grad, w_up)
    own_gain = lax.dynamic_slice_in_dim(norm_gain, mp_start, part_width)
    own_normed = lax.psum_scatter(
        normed_grad.astype(jnp.bfloat16), "mp", scatter_dimension=1, tiled=True
    ).astype(jnp.float32)
    inner_part = jnp.sum(own_input * own_gain[None, :] * own_normed, axis=1)
    inner = lax.psum(inner_part, "mp") / model_width
    input_grad = (
        own_out_grad
        + rms_scale * own_gain[None, :] * own_normed
        - own_input * rms_scale**3 * inner[:, None]
    )
    input_half = input_grad.astype(jnp.bfloat16).reshape(slot_capacity, block_len * part_width)
    back = jnp.dot(packed_half_rows.T, input_half, preferred_element_type=jnp.float32).astype(
        jnp.bfloat16
    )
    back_got = lax.all_to_all(
        back.reshape(dp_count, slot_count, block_len * part_width),
        "dp",
        split_axis=0,
        concat_axis=0,
        tiled=True,
    )
    grad_rows = jnp.dot(
        select_half.T,
        back_got.reshape(received, block_len * part_width),
        preferred_element_type=jnp.float32,
    )
    return (query_loss, grad_rows.astype(jnp.bfloat16).reshape(row_count, part_width))


def solution(mesh):
    return jax.shard_map(
        per_device,
        mesh=mesh,
        in_specs=(
            P("dp", "mp"),
            P("dp"),
            P("dp"),
            P("dp"),
            P("dp", "mp"),
            P(),
            P(None, "mp"),
            P(None, "mp"),
            P("mp", None),
        ),
        out_specs=(P("dp"), P("dp", "mp")),
        check_vma=False,
    )
```

profile of v0, /device:TPU:1, one launch (start us, length us, event | category | flops | bytes accessed | tf_op | source)
XLA Modules:
  0.0 400.2 jit_solution(1453509648983306713)
XLA Ops:
  7.2 0.7 broadcast_in_dim.17
  8.2 1.2 dynamic-slice
  10.1 0.9 dynamic-update-slice
  11.0 15.5 %all-reduce = s32[64]{0:T(128)S(1)} all-reduce(s32[64]{0:T(128)S(1)} %dynamic-update-slice), channel_id=1, replica_groups=mesh['dp'=32,'mp'=4] {'dp'}, use_global_device_ids=true, to_apply=%add | all-reduce | flops 64 | bytes 512
  26.5 0.6 fusion.66
  28.3 0.7 copy.74
  29.0 7.5 %all-to-all-start = ((bf16[32,1,1]{2,1,0:T(2,128)(2,1)}), bf16[32,1,1]{2,1,0:T(2,128)(2,1)S(1)}, u32[]{:S(2)}, u32[]{:S(2)}) async-start(bf16[32,1,1]{2,1,0:T(2,128)(2,1)} %copy.74), calls=%async_computation | async-start | bytes 32768 | tf_op jit(solution)/shard_map/all_to_all | solution.py:128
  36.4 1.6 reshape.442
  38.4 1.3 copy.91
  39.7 3.7 all-to-all-done
  43.5 4.2 %all-to-all-start.1 = ((bf16[32,1,32,512]{3,2,1,0:T(8,128)(2,1)}), bf16[32,1,32,512]{3,2,1,0:T(8,128)(2,1)S(1)}, u32[]{:S(2)}, u32[]{:S(2)}) async-start(bf16[32,1,32,512]{3,2,1,0:T(8,128)(2,1)} %bitcast.5), calls=%async_computation.1 | async-start | bytes 2097152 | tf_op jit(solution)/shard_map/all_to_all | solution.py:126
  48.0 0.6 copy.77
  49.2 15.6 %all-to-all-done.1 = bf16[32,1,32,512]{3,2,1,0:T(8,128)(2,1)S(1)} async-done(((bf16[32,1,32,512]{3,2,1,0:T(8,128)(2,1)}), bf16[32,1,32,512]{3,2,1,0:T(8,128)(2,1)S(1)}, u32[]{:S(2)}, u32[]{:S(2)}) %all-to-all-start.1) | async-done | bytes 1048608 | tf_op jit(solution)/shard_map/all_to_all | solution.py:126
  64.7 3.9 all-to-all-start.2
  68.7 0.6 copy.92
  69.3 1.6 fusion.82
  71.6 4.0 %all-to-all-done.2 = bf16[32,1,32]{2,1,0:T(2,128)(2,1)S(1)} async-done(((bf16[32,1,32]{2,1,0:T(2,128)(2,1)}), bf16[32,1,32]{2,1,0:T(2,128)(2,1)S(1)}, u32[]{:S(2)}, u32[]{:S(2)}) %all-to-all-start.2) | async-done | bytes 2080 | tf_op jit(solution)/shard_map/all_to_all | solution.py:127
  75.6 1.7 broadcast_in_dim.18
  77.3 4.8 %all-to-all-start.3 = ((bf16[4,640,512]{1,2,0:T(8,128)(2,1)}), bf16[4,640,512]{1,2,0:T(8,128)(2,1)S(1)}, u32[]{:S(2)}, u32[]{:S(2)}) async-start(bf16[4,640,512]{1,2,0:T(8,128)(2,1)} %broadcast_in_dim.18), calls=%async_computation.3 | async-start | bytes 5242880 | tf_op jit(solution)/shard_map/all_to_all | solution.py:17
  83.0 3.5 copy.93
  86.4 26.3 %all-to-all-done.3 = bf16[4,640,512]{1,2,0:T(8,128)(2,1)S(1)} async-done(((bf16[4,640,512]{1,2,0:T(8,128)(2,1)}), bf16[4,640,512]{1,2,0:T(8,128)(2,1)S(1)}, u32[]{:S(2)}, u32[]{:S(2)}) %all-to-all-start.3) | async-done | bytes 2621472 | tf_op jit(solution)/shard_map/all_to_all | solution.py:17
  112.7 0.6 multiply_reduce_fusion.1
  113.3 0.6 fusion.2
  114.0 8.6 %fusion.85 = f32[640,1792]{1,0:T(8,128)S(1)} fusion(bf16[640,2048]{0,1:T(8,128)(2,1)S(1)} %fusion.2, bf16[2048,1792]{1,0:T(8,128)(2,1)} %param.16), kind=kOutput, calls=%fused_computation.172 | convolution fusion | flops 4697620480 | bytes 14548992 | tf_op jit(solution)/shard_map/dot_general | solution.py:144
  122.7 5.4 %fusion.84 = f32[640,1792]{1,0:T(8,128)S(1)} fusion(bf16[640,2048]{0,1:T(8,128)(2,1)S(1)} %fusion.2, bf16[2048,1792]{1,0:T(8,128)(2,1)S(1)} %bitcast.102), kind=kOutput, calls=%fused_computation.171 | convolution fusion | flops 4697620480 | bytes 14548992 | tf_op jit(solution)/shard_map/dot_general | solution.py:143
  128.2 5.0 %fusion.4 = f32[640,2048]{1,0:T(8,128)S(1)} fusion(bf16[1792,2048]{1,0:T(8,128)(2,1)S(1)} %bitcast.100, f32[640,1792]{1,0:T(8,128)S(1)} %fusion.85, f32[640,1792]{1,0:T(8,128)S(1)} %fusion.84), kind=kOutput, calls=%fused_computation.17 | convolution fusion | flops 4704501760 | bytes 21757952 | tf_op jit(solution)/shard_map/dot_general | solution.py:147
  133.2 1.0 multiply_reduce_fusion
  134.2 0.7 copy.79
  134.9 3.3 all-to-all-start.4
  138.5 4.3 %all-to-all-done.4 = bf16[4,20,512]{2,1,0:T(8,128)(2,1)S(1)} async-done(((bf16[4,20,512]{2,1,0:T(8,128)(2,1)}), bf16[4,20,512]{2,1,0:T(8,128)(2,1)S(1)}, u32[]{:S(2)}, u32[]{:S(2)}) %all-to-all-start.4) | async-done | bytes 81952 | tf_op jit(solution)/shard_map/all_to_all | solution.py:38
  143.5 0.7 reduce.13
  144.2 0.6 reshape.475
  144.8 6.5 %all-to-all-start.5 = ((bf16[32,2,256]{2,1,0:T(2,128)(2,1)}), bf16[32,2,256]{2,1,0:T(2,128)(2,1)S(1)}, u32[]{:S(2)}, u32[]{:S(2)}) async-start(bf16[32,2,256]{2,1,0:T(2,128)(2,1)} %reshape.475), calls=%async_computation.5 | async-start | bytes 65536 | tf_op jit(solution)/shard_map/all_to_all | solution.py:159
  151.6 7.1 %all-to-all-done.5 = bf16[32,2,256]{2,1,0:T(2,128)(2,1)S(1)} async-done(((bf16[32,2,256]{2,1,0:T(2,128)(2,1)}), bf16[32,2,256]{2,1,0:T(2,128)(2,1)S(1)}, u32[]{:S(2)}, u32[]{:S(2)}) %all-to-all-start.5) | async-done | bytes 32800 | tf_op jit(solution)/shard_map/all_to_all | solution.py:159
  159.0 23.1 %all_gather.10 = bf16[256,512]{1,0:T(8,128)(2,1)S(1)} all-gather(bf16[8,512]{1,0:T(8,128)(2,1)S(1)} %divide_convert_fusion), channel_id=1, replica_groups=mesh['dp'=32,'mp'=4] {'dp'}, dimensions={0}, use_global_device_ids=true | all-gather | bytes 270336 | tf_op jit(solution)/shard_map/all_gather | solution.py:173
  182.2 0.9 fusion.15
  183.1 6.9 %all-reduce.1 = (bf16[256]{0:T(256)(128)(2,1)S(1)}, bf16[128]{0:T(256)(128)(2,1)S(1)}) all-reduce(bf16[256]{0:T(256)(128)(2,1)S(1)} %multiply_reduce_fusion.2, bf16[128]{0:T(256)(128)(2,1)S(1)} %multiply_reduce_fusion.3), channel_id=1, replica_groups=mesh['dp'=32,'mp'=4] {'mp'}, use_global_device_ids=true, to_apply=%region_15.16 | all-reduce | flops 384 | bytes 1536 | tf_op jit(solution)/shard_map/psum | solution.py:183
  190.0 37.0 %all-reduce.4.cloned.1.call-done = bf16[128,256]{0,1:T(8,128)(2,1)} async-done(((bf16[128,256]{0,1:T(8,128)(2,1)}), bf16[128,256]{0,1:T(8,128)(2,1)}) %all-reduce.4.cloned.1.call-update) | async-done | bytes 65552 | tf_op jit(solution)/shard_map/psum | solution.py:182
  227.0 1.0 fusion.78
  228.1 1.1 fusion.24
  229.4 1.1 fusion.14
  230.5 0.8 pad_maximum_fusion
  231.3 9.7 %all-to-all-start.6 = ((bf16[32,8,513]{2,1,0:T(8,128)(2,1)}), bf16[32,8,513]{2,1,0:T(8,128)(2,1)S(1)}, u32[]{:S(2)}, u32[]{:S(2)}) async-start(bf16[32,8,513]{2,1,0:T(8,128)(2,1)} %pad_maximum_fusion), calls=%async_computation.6 | async-start | bytes 655360 | tf_op jit(solution)/shard_map/all_to_all | solution.py:38
  241.0 9.6 %all-to-all-done.6 = bf16[32,8,513]{2,1,0:T(8,128)(2,1)S(1)} async-done(((bf16[32,8,513]{2,1,0:T(8,128)(2,1)}), bf16[32,8,513]{2,1,0:T(8,128)(2,1)S(1)}, u32[]{:S(2)}, u32[]{:S(2)}) %all-to-all-start.6) | async-done | bytes 262688 | tf_op jit(solution)/shard_map/all_to_all | solution.py:38
  251.2 0.7 reduce.14
  251.8 0.6 reshape.477
  252.5 3.6 all-to-all-start.7
  256.2 7.1 %all-to-all-done.7 = bf16[32,2,256]{2,1,0:T(2,128)(2,1)S(1)} async-done(((bf16[32,2,256]{2,1,0:T(2,128)(2,1)}), bf16[32,2,256]{2,1,0:T(2,128)(2,1)S(1)}, u32[]{:S(2)}, u32[]{:S(2)}) %all-to-all-start.7) | async-done | bytes 32800 | tf_op jit(solution)/shard_map/all_to_all | solution.py:228
  263.5 9.0 %all_gather.11 = bf16[20,2048]{1,0:T(8,128)(2,1)S(1)} all-gather(bf16[20,512]{1,0:T(8,128)(2,1)S(1)} %get-tuple-element.20), channel_id=1, replica_groups=mesh['dp'=32,'mp'=4] {'mp'}, dimensions={1}, use_global_device_ids=true | all-gather | bytes 102400 | tf_op jit(solution)/shard_map/all_gather | solution.py:238
  272.9 10.2 %fusion.86 = f32[640,1792]{1,0:T(8,128)} fusion(bf16[640,2048]{1,0:T(8,128)(2,1)S(1)} %fusion.3, bf16[1792,2048]{1,0:T(8,128)(2,1)} %param.17), kind=kOutput, calls=%fused_computation.173 | convolution fusion | flops 4697620480 | bytes 14548992 | tf_op jit(solution)/shard_map/dot_general | solution.py:55
  283.1 14.2 %fusion.7 = f32[640,2048]{1,0:T(8,128)} fusion(bf16[2048,1792]{1,0:T(8,128)(2,1)S(1)} %bitcast.104, f32[640,1792]{1,0:T(8,128)} %copy-done.6, f32[640,1792]{1,0:T(8,128)} %fusion.86, f32[640,1792]{1,0:T(8,128)} %copy-done.7), kind=kOutput, calls=%fused_computation.20 | convolution fusion | flops 4709089280 | bytes 26345472 | tf_op jit(solution)/shard_map/dot_general | solution.py:55
  297.4 13.7 %add_convert_fusion = bf16[640,2048]{1,0:T(8,128)(2,1)} fusion(f32[640,2048]{1,0:T(8,128)} %fusion.7, bf16[2048,1792]{1,0:T(8,128)(2,1)} %param.16, f32[640,1792]{1,0:T(8,128)} %fusion.86, f32[640,1792]{1,0:T(8,128)} %copy-done.6), kind=kOutput, calls=%fused_computation.10 | convolution fusion | flops 4707123200 | bytes 24379392 | tf_op jit(solution)/shard_map/dot_general | solution.py:55
  311.1 32.8 %reduce-scatter.2.cloned.1.call-done = bf16[640,512]{1,0:T(8,128)(2,1)} async-done(((bf16[640,2048]{1,0:T(8,128)(2,1)}), bf16[640,512]{1,0:T(8,128)(2,1)}) %reduce-scatter.2.cloned.1.call-update) | async-done | bytes 655376 | tf_op jit(solution)/shard_map/reduce_scatter | solution.py:254
  343.9 1.4 fusion.11
  345.3 6.5 %psum.31 = f32[640]{0:T(1024)S(1)} all-reduce(f32[640]{0:T(1024)S(1)} %fusion.11), channel_id=1, replica_groups=mesh['dp'=32,'mp'=4] {'mp'}, use_global_device_ids=true, to_apply=%region_23.24 | all-reduce | flops 640 | bytes 5120 | tf_op jit(solution)/shard_map/psum | solution.py:258
  351.8 1.6 fusion.10
  354.3 1.4 reduce.15
  355.7 1.6 reshape.479
  357.3 9.7 %all-to-all-start.8 = ((bf16[32,2,8192]{2,1,0:T(2,128)(2,1)}), bf16[32,2,8192]{2,1,0:T(2,128)(2,1)}, u32[]{:S(2)}, u32[]{:S(2)}) async-start(bf16[32,2,8192]{2,1,0:T(2,128)(2,1)} %reshape.479), calls=%async_computation.9 | async-start | bytes 2097152 | tf_op jit(solution)/shard_map/all_to_all | solution.py:268
  367.0 0.5 log_subtract_fusion
  367.6 16.4 %all-to-all-done.8 = bf16[32,2,8192]{2,1,0:T(2,128)(2,1)} async-done(((bf16[32,2,8192]{2,1,0:T(2,128)(2,1)}), bf16[32,2,8192]{2,1,0:T(2,128)(2,1)}, u32[]{:S(2)}, u32[]{:S(2)}) %all-to-all-start.8) | async-done | bytes 1048608 | tf_op jit(solution)/shard_map/all_to_all | solution.py:268
  384.0 4.3 %reshape.480 = bf16[32,1,16384]{2,1,0:T(2,128)(2,1)S(1)} reshape(bf16[32,2,8192]{2,1,0:T(2,128)(2,1)} %all-to-all-done.8) | data formatting | bytes 2097152
  388.3 2.5 convolution_convert_fusion
  390.8 2.3 reshape.459
  (105 shorter events, 7.9 us)
Async XLA Ops:
  7.2 40.6 %copy-start.3 = (s32[1024]{0:T(1024)S(1)}, s32[1024]{0:T(1024)}, u32[]{:S(2)}) copy-start(s32[1024]{0:T(1024)} %param.10) | copy-start | bytes 12292
  29.0 14.5 %all-to-all-start = ((bf16[32,1,1]{2,1,0:T(2,128)(2,1)}), bf16[32,1,1]{2,1,0:T(2,128)(2,1)S(1)}, u32[]{:S(2)}, u32[]{:S(2)}) async-start(bf16[32,1,1]{2,1,0:T(2,128)(2,1)} %copy.74), calls=%async_computation | async-start | bytes 32768 | tf_op jit(solution)/shard_map/all_to_all | solution.py:128
  43.5 21.2 %all-to-all-start.1 = ((bf16[32,1,32,512]{3,2,1,0:T(8,128)(2,1)}), bf16[32,1,32,512]{3,2,1,0:T(8,128)(2,1)S(1)}, u32[]{:S(2)}, u32[]{:S(2)}) async-start(bf16[32,1,32,512]{3,2,1,0:T(8,128)(2,1)} %bitcast.5), calls=%async_computation.1 | async-start | bytes 2097152 | tf_op jit(solution)/shard_map/all_to_all | solution.py:126
  64.7 10.9 %all-to-all-start.2 = ((bf16[32,1,32]{2,1,0:T(2,128)(2,1)}), bf16[32,1,32]{2,1,0:T(2,128)(2,1)S(1)}, u32[]{:S(2)}, u32[]{:S(2)}) async-start(bf16[32,1,32]{2,1,0:T(2,128)(2,1)} %copy.77), calls=%async_computation.2 | async-start | bytes 32768 | tf_op jit(solution)/shard_map/all_to_all | solution.py:127
  71.6 10.6 %copy-start.5 = (s32[2]{0:T(128)S(1)}, s32[2]{0:T(128)}, u32[]{:S(2)}) copy-start(s32[2]{0:T(128)} %param.11) | copy-start | bytes 28
  71.6 11.2 %copy-start.4 = (s32[128]{0:T(128)S(1)}, s32[128]{0:T(128)}, u32[]{:S(2)}) copy-start(s32[128]{0:T(128)} %param.12) | copy-start | bytes 1540
  77.3 36.0 %copy-start.2 = (f32[2048]{0:T(1024)S(1)}, f32[2048]{0:T(1024)}, u32[]{:S(2)}) copy-start(f32[2048]{0:T(1024)} %param.14) | copy-start | bytes 24580
  77.3 35.4 %all-to-all-start.3 = ((bf16[4,640,512]{1,2,0:T(8,128)(2,1)}), bf16[4,640,512]{1,2,0:T(8,128)(2,1)S(1)}, u32[]{:S(2)}, u32[]{:S(2)}) async-start(bf16[4,640,512]{1,2,0:T(8,128)(2,1)} %broadcast_in_dim.18), calls=%async_computation.3 | async-start | bytes 5242880 | tf_op jit(solution)/shard_map/all_to_all | solution.py:17
  113.3 9.3 %slice-start.2 = ((s8[7340032]{0:T(1024)(128)(4,1)}), s8[4194304]{0:T(1024)(128)(4,1)S(1)}, s32[]{:S(2)}) async-start(s8[7340032]{0:T(1024)(128)(4,1)} %bitcast.101), calls=%async_computation.14 | async-start | bytes 8388608
  113.3 14.8 %slice-start = ((s8[7340032]{0:T(1024)(128)(4,1)}), s8[4194304]{0:T(1024)(128)(4,1)S(1)}, s32[]{:S(2)}) async-start(s8[7340032]{0:T(1024)(128)(4,1)} %bitcast.99), calls=%async_computation.12 | async-start | bytes 8388608
  114.0 8.7 %slice-start.3 = ((s8[7340032]{0:T(1024)(128)(4,1)}), s8[3145728]{0:T(1024)(128)(4,1)S(1)}, s32[]{:S(2)}) async-start(s8[7340032]{0:T(1024)(128)(4,1)} %bitcast.101), calls=%async_computation.15 | async-start | bytes 6291456
  114.0 14.2 %slice-start.1 = ((s8[7340032]{0:T(1024)(128)(4,1)}), s8[3145728]{0:T(1024)(128)(4,1)S(1)}, s32[]{:S(2)}) async-start(s8[7340032]{0:T(1024)(128)(4,1)} %bitcast.99), calls=%async_computation.13 | async-start | bytes 6291456
  122.7 5.5 %copy-start.7 = (f32[640,1792]{1,0:T(8,128)}, f32[640,1792]{1,0:T(8,128)S(1)}, u32[]{:S(2)}) copy-start(f32[640,1792]{1,0:T(8,128)S(1)} %fusion.85) | copy-start | bytes 13762564
  128.2 5.0 %copy-start.6 = (f32[640,1792]{1,0:T(8,128)}, f32[640,1792]{1,0:T(8,128)S(1)}, u32[]{:S(2)}) copy-start(f32[640,1792]{1,0:T(8,128)S(1)} %fusion.84) | copy-start | bytes 13762564
  133.2 5.0 %copy-start = (f32[3,8,32,512]{3,2,1,0:T(8,128)S(1)}, f32[3,8,32,512]{3,2,1,0:T(8,128)}, u32[]{:S(2)}) copy-start(f32[3,8,32,512]{3,2,1,0:T(8,128)} %copy.93) | copy-start | bytes 4718596
  133.2 18.2 %copy-start.1 = (bf16[128,512]{1,0:T(8,128)(2,1)S(1)}, bf16[128,512]{1,0:T(8,128)(2,1)}, u32[]{:S(2)}) copy-start(bf16[128,512]{1,0:T(8,128)(2,1)} %param.13) | copy-start | bytes 393220
  134.9 7.9 %all-to-all-start.4 = ((bf16[4,20,512]{2,1,0:T(8,128)(2,1)}), bf16[4,20,512]{2,1,0:T(8,128)(2,1)S(1)}, u32[]{:S(2)}, u32[]{:S(2)}) async-start(bf16[4,20,512]{2,1,0:T(8,128)(2,1)} %copy.79), calls=%async_computation.4 | async-start | bytes 196608 | tf_op jit(solution)/shard_map/all_to_all | solution.py:38
  144.8 13.9 %all-to-all-start.5 = ((bf16[32,2,256]{2,1,0:T(2,128)(2,1)}), bf16[32,2,256]{2,1,0:T(2,128)(2,1)S(1)}, u32[]{:S(2)}, u32[]{:S(2)}) async-start(bf16[32,2,256]{2,1,0:T(2,128)(2,1)} %reshape.475), calls=%async_computation.5 | async-start | bytes 65536 | tf_op jit(solution)/shard_map/all_to_all | solution.py:159
  151.3 75.6 %all-reduce.4.cloned.1.call-start = ((), (), s32[]{:S(2)}) async-start(), calls=%async_computation.10 | async-start | bytes 131072 | tf_op jit(solution)/shard_map/psum | solution.py:182
  231.3 19.3 %all-to-all-start.6 = ((bf16[32,8,513]{2,1,0:T(8,128)(2,1)}), bf16[32,8,513]{2,1,0:T(8,128)(2,1)S(1)}, u32[]{:S(2)}, u32[]{:S(2)}) async-start(bf16[32,8,513]{2,1,0:T(8,128)(2,1)} %pad_maximum_fusion), calls=%async_computation.6 | async-start | bytes 655360 | tf_op jit(solution)/shard_map/all_to_all | solution.py:38
  252.5 10.9 %all-to-all-start.7 = ((bf16[32,2,256]{2,1,0:T(2,128)(2,1)}), bf16[32,2,256]{2,1,0:T(2,128)(2,1)S(1)}, u32[]{:S(2)}, u32[]{:S(2)}) async-start(bf16[32,2,256]{2,1,0:T(2,128)(2,1)} %reshape.477), calls=%async_computation.7 | async-start | bytes 65536 | tf_op jit(solution)/shard_map/all_to_all | solution.py:228
  256.1 87.8 %reduce-scatter.2.cloned.1.call-start = ((), (), s32[]{:S(2)}) async-start(), calls=%async_computation.11 | async-start | bytes 3276800 | tf_op jit(solution)/shard_map/reduce_scatter | solution.py:254
  272.6 10.5 %slice-start.4 = ((s8[7340032]{0:T(1024)(128)(4,1)}), s8[4194304]{0:T(1024)(128)(4,1)S(1)}, s32[]{:S(2)}) async-start(s8[7340032]{0:T(1024)(128)(4,1)} %bitcast.103), calls=%async_computation.16 | async-start | bytes 8388608
  272.9 10.2 %slice-start.5 = ((s8[7340032]{0:T(1024)(128)(4,1)}), s8[3145728]{0:T(1024)(128)(4,1)S(1)}, s32[]{:S(2)}) async-start(s8[7340032]{0:T(1024)(128)(4,1)} %bitcast.103), calls=%async_computation.17 | async-start | bytes 6291456
  357.3 26.7 %all-to-all-start.8 = ((bf16[32,2,8192]{2,1,0:T(2,128)(2,1)}), bf16[32,2,8192]{2,1,0:T(2,128)(2,1)}, u32[]{:S(2)}, u32[]{:S(2)}) async-start(bf16[32,2,8192]{2,1,0:T(2,128)(2,1)} %reshape.479), calls=%async_computation.9 | async-start | bytes 2097152 | tf_op jit(solution)/shard_map/all_to_all | solution.py:268
Sparse Core Ops, SparseCore 0:
  190.1 36.8 all-reduce.3
  311.2 32.6 reduce-scatter.1
where the time goes:
time: 406 us; the launch traced here: 400 us
  waiting for transfers between devices  164 us (40%)
  matrix products  65.1 us (16%)
  blocking collectives  61 us (15%)
  starting transfers between devices  53.3 us (13%)
  local copies, waits for them, and re-layouts  26.3 us (6%)
  between operations  16.1 us (4%)
  other arithmetic  14.4 us (4%)
    dot_general x4, matrix products, contract_rows(): lax.dot_general(left, right, (((1,), (1,)), ((), ())), preferred_element_...  38.9 us
    psum x1, waiting for transfers between devices, per_device(): lax.psum(score_part.astype(jnp.bfloat16), 'mp').astype(jnp.float32)  37 us
    reduce_scatter x1, waiting for transfers between devices, per_device(): lax.psum_scatter(normed_grad.astype(jnp.bfloat16), 'mp', scatter_dimensio...  32.8 us
    all_to_all x1, waiting for transfers between devices, sent_to_all(): return lax.all_to_all(copies, axis, split_axis=0, concat_axis=0, tiled=True)  26.3 us
    all_gather x1, blocking collectives, per_device(): all_vec = lax.all_gather(passage_vec, 'dp', axis=0, tiled=True)  23.1 us
    all_to_all x1, waiting for transfers between devices, per_device(): lax.all_to_all(back.reshape(dp_count, slot_count, block_len * part_width)...  16.4 us
    all_to_all x1, waiting for transfers between devices, per_device(): lax.all_to_all(send, 'dp', split_axis=0, concat_axis=0, tiled=True)  15.6 us
    unnamed x1, blocking collectives  15.5 us
  transfers between devices with their start and end apart: 11, of which 11 were waited for; matrix products, arithmetic and copies ran while one was open for 3% of the time, Pallas kernels for 0%

commit v1 on v0

--- a/solution.py
+++ b/solution.py
@@ -179,7 +179,7 @@
     query_float = queries.astype(jnp.float32)
     score_part = contract_rows(queries, all_vec)
     raw_score, passage_sq, query_sq = (
-        lax.psum(score_part.astype(jnp.bfloat16), "mp").astype(jnp.float32),
+        jnp.sum(lax.all_gather(score_part.astype(jnp.bfloat16), "mp"), axis=0).astype(jnp.float32),
         lax.psum(jnp.sum(vec_float * vec_float, axis=1).astype(jnp.bfloat16), "mp").astype(
             jnp.float32
         ),

time: 406 us -> 374 us (0.921)
  waiting for transfers between devices: 164 us -> 127 us
  blocking collectives: 61 us -> 70.7 us
    psum x1 -> x0, waiting for transfers between devices: 37 us -> none  [per_device(): lax.psum(score_part.astype(jnp.bfloat16), 'mp').astype(jnp.float32)]
    all_gather x0 -> x1, blocking collectives: none -> 9.66 us  [per_device(): lax.all_gather(score_part.astype(jnp.bfloat16), 'mp')]
  transfers between devices with their start and end apart: 11 -> 10, of which waited for: 11 -> 10; matrix products, arithmetic and copies ran while one was open for 3% -> 4% of each run, Pallas kernels for 0% -> 0%
where the time goes in v1:
time: 374 us; the launch traced here: 369 us
  waiting for transfers between devices  127 us (34%)
  blocking collectives  70.7 us (19%)
  matrix products  63.7 us (17%)
  starting transfers between devices  51.6 us (14%)
  local copies, waits for them, and re-layouts  26.7 us (7%)
  between operations  16.2 us (4%)
  other arithmetic  13.2 us (4%)
    dot_general x4, matrix products, contract_rows(): lax.dot_general(left, right, (((1,), (1,)), ((), ())), preferred_element_...  38.3 us
    reduce_scatter x1, waiting for transfers between devices, per_device(): lax.psum_scatter(normed_grad.astype(jnp.bfloat16), 'mp', scatter_dimensio...  32.7 us
    all_to_all x1, waiting for transfers between devices, sent_to_all(): return lax.all_to_all(copies, axis, split_axis=0, concat_axis=0, tiled=True)  26.1 us
    all_gather x1, blocking collectives, per_device(): all_vec = lax.all_gather(passage_vec, 'dp', axis=0, tiled=True)  23.1 us
    all_to_all x1, waiting for transfers between devices, per_device(): lax.all_to_all(back.reshape(dp_count, slot_count, block_len * part_width)...  16.4 us
    all_to_all x1, waiting for transfers between devices, per_device(): lax.all_to_all(send, 'dp', split_axis=0, concat_axis=0, tiled=True)  15.6 us
    unnamed x1, blocking collectives  15.5 us
    unnamed x40, local copies, waits for them, and re-layouts  14.7 us
  transfers between devices with their start and end apart: 10, of which 10 were waited for; matrix products, arithmetic and copies ran while one was open for 4% of the time, Pallas kernels for 0%

profile of v1, /device:TPU:1, one launch (start us, length us, event | category | flops | bytes accessed | tf_op | source)
XLA Modules:
  0.0 368.7 jit_solution(273915215792105993)
XLA Ops:
  7.2 0.7 broadcast_in_dim.20
  8.2 1.2 dynamic-slice
  10.1 0.9 dynamic-update-slice
  11.0 15.5 %all-reduce = s32[64]{0:T(128)S(1)} all-reduce(s32[64]{0:T(128)S(1)} %dynamic-update-slice), channel_id=1, replica_groups=mesh['dp'=32,'mp'=4] {'dp'}, use_global_device_ids=true, to_apply=%add | all-reduce | flops 64 | bytes 512
  26.5 0.6 fusion.69
  28.3 0.7 copy.74
  29.0 7.5 %all-to-all-start = ((bf16[32,1,1]{2,1,0:T(2,128)(2,1)}), bf16[32,1,1]{2,1,0:T(2,128)(2,1)S(1)}, u32[]{:S(2)}, u32[]{:S(2)}) async-start(bf16[32,1,1]{2,1,0:T(2,128)(2,1)} %copy.74), calls=%async_computation | async-start | bytes 32768 | tf_op jit(solution)/shard_map/all_to_all | solution.py:128
  36.4 1.6 reshape.533
  38.0 0.5 convolution_convert_fusion.2
  38.4 1.3 copy.91
  39.7 3.7 %all-to-all-done = bf16[32,1,1]{2,1,0:T(2,128)(2,1)S(1)} async-done(((bf16[32,1,1]{2,1,0:T(2,128)(2,1)}), bf16[32,1,1]{2,1,0:T(2,128)(2,1)S(1)}, u32[]{:S(2)}, u32[]{:S(2)}) %all-to-all-start) | async-done | bytes 96 | tf_op jit(solution)/shard_map/all_to_all | solution.py:128
  43.5 4.2 %all-to-all-start.1 = ((bf16[32,1,32,512]{3,2,1,0:T(8,128)(2,1)}), bf16[32,1,32,512]{3,2,1,0:T(8,128)(2,1)S(1)}, u32[]{:S(2)}, u32[]{:S(2)}) async-start(bf16[32,1,32,512]{3,2,1,0:T(8,128)(2,1)} %bitcast.5), calls=%async_computation.1 | async-start | bytes 2097152 | tf_op jit(solution)/shard_map/all_to_all | solution.py:126
  48.0 0.6 copy.77
  49.2 15.6 %all-to-all-done.1 = bf16[32,1,32,512]{3,2,1,0:T(8,128)(2,1)S(1)} async-done(((bf16[32,1,32,512]{3,2,1,0:T(8,128)(2,1)}), bf16[32,1,32,512]{3,2,1,0:T(8,128)(2,1)S(1)}, u32[]{:S(2)}, u32[]{:S(2)}) %all-to-all-start.1) | async-done | bytes 1048608 | tf_op jit(solution)/shard_map/all_to_all | solution.py:126
  64.7 3.9 %all-to-all-start.2 = ((bf16[32,1,32]{2,1,0:T(2,128)(2,1)}), bf16[32,1,32]{2,1,0:T(2,128)(2,1)S(1)}, u32[]{:S(2)}, u32[]{:S(2)}) async-start(bf16[32,1,32]{2,1,0:T(2,128)(2,1)} %copy.77), calls=%async_computation.2 | async-start | bytes 32768 | tf_op jit(solution)/shard_map/all_to_all | solution.py:127
  68.7 0.6 copy.92
  69.3 1.6 fusion.84
  70.8 0.4 reshape.538
  71.6 4.0 %all-to-all-done.2 = bf16[32,1,32]{2,1,0:T(2,128)(2,1)S(1)} async-done(((bf16[32,1,32]{2,1,0:T(2,128)(2,1)}), bf16[32,1,32]{2,1,0:T(2,128)(2,1)S(1)}, u32[]{:S(2)}, u32[]{:S(2)}) %all-to-all-start.2) | async-done | bytes 2080 | tf_op jit(solution)/shard_map/all_to_all | solution.py:127
  75.6 1.7 broadcast_in_dim.21
  77.3 4.8 %all-to-all-start.3 = ((bf16[4,640,512]{1,2,0:T(8,128)(2,1)}), bf16[4,640,512]{1,2,0:T(8,128)(2,1)S(1)}, u32[]{:S(2)}, u32[]{:S(2)}) async-start(bf16[4,640,512]{1,2,0:T(8,128)(2,1)} %broadcast_in_dim.21), calls=%async_computation.3 | async-start | bytes 5242880 | tf_op jit(solution)/shard_map/all_to_all | solution.py:17
  83.2 3.5 copy.93
  86.6 26.1 %all-to-all-done.3 = bf16[4,640,512]{1,2,0:T(8,128)(2,1)S(1)} async-done(((bf16[4,640,512]{1,2,0:T(8,128)(2,1)}), bf16[4,640,512]{1,2,0:T(8,128)(2,1)S(1)}, u32[]{:S(2)}, u32[]{:S(2)}) %all-to-all-start.3) | async-done | bytes 2621472 | tf_op jit(solution)/shard_map/all_to_all | solution.py:17
  112.7 0.6 multiply_reduce_fusion.1
  113.3 0.6 fusion.2
  114.0 8.6 %fusion.87 = f32[640,1792]{1,0:T(8,128)S(1)} fusion(bf16[640,2048]{0,1:T(8,128)(2,1)S(1)} %fusion.2, bf16[2048,1792]{1,0:T(8,128)(2,1)} %param.16), kind=kOutput, calls=%fused_computation.180 | convolution fusion | flops 4697620480 | bytes 14548992 | tf_op jit(solution)/shard_map/dot_general | solution.py:144
  122.7 5.4 %fusion.86 = f32[640,1792]{1,0:T(8,128)S(1)} fusion(bf16[640,2048]{0,1:T(8,128)(2,1)S(1)} %fusion.2, bf16[2048,1792]{1,0:T(8,128)(2,1)S(1)} %bitcast.105), kind=kOutput, calls=%fused_computation.179 | convolution fusion | flops 4697620480 | bytes 14548992 | tf_op jit(solution)/shard_map/dot_general | solution.py:143
  128.2 5.0 %fusion.4 = f32[640,2048]{1,0:T(8,128)S(1)} fusion(bf16[1792,2048]{1,0:T(8,128)(2,1)S(1)} %bitcast.103, f32[640,1792]{1,0:T(8,128)S(1)} %fusion.87, f32[640,1792]{1,0:T(8,128)S(1)} %fusion.86), kind=kOutput, calls=%fused_computation.17 | convolution fusion | flops 4704501760 | bytes 21757952 | tf_op jit(solution)/shard_map/dot_general | solution.py:147
  133.2 1.0 multiply_reduce_fusion
  134.2 0.7 copy.79
  134.9 3.3 all-to-all-start.4
  138.5 4.3 %all-to-all-done.4 = bf16[4,20,512]{2,1,0:T(8,128)(2,1)S(1)} async-done(((bf16[4,20,512]{2,1,0:T(8,128)(2,1)}), bf16[4,20,512]{2,1,0:T(8,128)(2,1)S(1)}, u32[]{:S(2)}, u32[]{:S(2)}) %all-to-all-start.4) | async-done | bytes 81952 | tf_op jit(solution)/shard_map/all_to_all | solution.py:38
  143.0 0.5 broadcast.550
  143.5 0.7 reduce.18
  144.2 0.6 reshape.567
  144.8 6.5 %all-to-all-start.5 = ((bf16[32,2,256]{2,1,0:T(2,128)(2,1)}), bf16[32,2,256]{2,1,0:T(2,128)(2,1)S(1)}, u32[]{:S(2)}, u32[]{:S(2)}) async-start(bf16[32,2,256]{2,1,0:T(2,128)(2,1)} %reshape.567), calls=%async_computation.5 | async-start | bytes 65536 | tf_op jit(solution)/shard_map/all_to_all | solution.py:159
  151.6 7.1 %all-to-all-done.5 = bf16[32,2,256]{2,1,0:T(2,128)(2,1)S(1)} async-done(((bf16[32,2,256]{2,1,0:T(2,128)(2,1)}), bf16[32,2,256]{2,1,0:T(2,128)(2,1)S(1)}, u32[]{:S(2)}, u32[]{:S(2)}) %all-to-all-start.5) | async-done | bytes 32800 | tf_op jit(solution)/shard_map/all_to_all | solution.py:159
  158.9 23.1 %all_gather.16 = bf16[256,512]{1,0:T(8,128)(2,1)S(1)} all-gather(bf16[8,512]{1,0:T(8,128)(2,1)S(1)} %divide_convert_fusion), channel_id=1, replica_groups=mesh['dp'=32,'mp'=4] {'dp'}, dimensions={0}, use_global_device_ids=true | all-gather | bytes 270336 | tf_op jit(solution)/shard_map/all_gather | solution.py:173
  182.4 6.9 %all-reduce.1 = (bf16[256]{0:T(256)(128)(2,1)S(1)}, bf16[128]{0:T(256)(128)(2,1)S(1)}) all-reduce(bf16[256]{0:T(256)(128)(2,1)S(1)} %multiply_reduce_fusion.2, bf16[128]{0:T(256)(128)(2,1)S(1)} %multiply_reduce_fusion.3), channel_id=1, replica_groups=mesh['dp'=32,'mp'=4] {'mp'}, use_global_device_ids=true, to_apply=%region_15.16 | all-reduce | flops 384 | bytes 1536 | tf_op jit(solution)/shard_map/psum | solution.py:183
  189.4 9.7 %all-gather = bf16[512,256]{0,1:T(8,128)(2,1)S(1)} all-gather(bf16[128,256]{0,1:T(8,128)(2,1)S(1)} %fusion.15), channel_id=2, replica_groups=mesh['dp'=32,'mp'=4] {'mp'}, dimensions={0}, use_global_device_ids=true | all-gather | bytes 327680 | tf_op jit(solution)/shard_map/all_gather | solution.py:182
  200.7 0.8 pad_maximum_fusion
  201.4 8.1 %all-to-all-start.6 = ((bf16[32,8,513]{2,1,0:T(8,128)(2,1)}), bf16[32,8,513]{2,1,0:T(8,128)(2,1)S(1)}, u32[]{:S(2)}, u32[]{:S(2)}) async-start(bf16[32,8,513]{2,1,0:T(8,128)(2,1)} %pad_maximum_fusion), calls=%async_computation.6 | async-start | bytes 655360 | tf_op jit(solution)/shard_map/all_to_all | solution.py:38
  209.5 9.6 %all-to-all-done.6 = bf16[32,8,513]{2,1,0:T(8,128)(2,1)S(1)} async-done(((bf16[32,8,513]{2,1,0:T(8,128)(2,1)}), bf16[32,8,513]{2,1,0:T(8,128)(2,1)S(1)}, u32[]{:S(2)}, u32[]{:S(2)}) %all-to-all-start.6) | async-done | bytes 262688 | tf_op jit(solution)/shard_map/all_to_all | solution.py:38
  219.7 0.7 reduce.19
  220.4 0.6 reshape.569
  221.0 3.6 all-to-all-start.7
  224.8 7.1 %all-to-all-done.7 = bf16[32,2,256]{2,1,0:T(2,128)(2,1)S(1)} async-done(((bf16[32,2,256]{2,1,0:T(2,128)(2,1)}), bf16[32,2,256]{2,1,0:T(2,128)(2,1)S(1)}, u32[]{:S(2)}, u32[]{:S(2)}) %all-to-all-start.7) | async-done | bytes 32800 | tf_op jit(solution)/shard_map/all_to_all | solution.py:228
  232.1 9.0 %all_gather.19 = bf16[20,2048]{1,0:T(8,128)(2,1)S(1)} all-gather(bf16[20,512]{1,0:T(8,128)(2,1)S(1)} %get-tuple-element.20), channel_id=1, replica_groups=mesh['dp'=32,'mp'=4] {'mp'}, dimensions={1}, use_global_device_ids=true | all-gather | bytes 102400 | tf_op jit(solution)/shard_map/all_gather | solution.py:238
  241.5 10.2 %fusion.88 = f32[640,1792]{1,0:T(8,128)} fusion(bf16[640,2048]{1,0:T(8,128)(2,1)S(1)} %fusion.3, bf16[1792,2048]{1,0:T(8,128)(2,1)} %param.17), kind=kOutput, calls=%fused_computation.181 | convolution fusion | flops 4697620480 | bytes 14548992 | tf_op jit(solution)/shard_map/dot_general | solution.py:55
  251.7 14.2 %fusion.7 = f32[640,2048]{1,0:T(8,128)} fusion(bf16[2048,1792]{1,0:T(8,128)(2,1)S(1)} %bitcast.107, f32[640,1792]{1,0:T(8,128)} %copy-done.6, f32[640,1792]{1,0:T(8,128)} %fusion.88, f32[640,1792]{1,0:T(8,128)} %copy-done.7), kind=kOutput, calls=%fused_computation.20 | convolution fusion | flops 4709089280 | bytes 26345472 | tf_op jit(solution)/shard_map/dot_general | solution.py:55
  265.9 13.7 %add_convert_fusion = bf16[640,2048]{1,0:T(8,128)(2,1)} fusion(f32[640,2048]{1,0:T(8,128)} %fusion.7, bf16[2048,1792]{1,0:T(8,128)(2,1)} %param.16, f32[640,1792]{1,0:T(8,128)} %fusion.88, f32[640,1792]{1,0:T(8,128)} %copy-done.6), kind=kOutput, calls=%fused_computation.10 | convolution fusion | flops 4707123200 | bytes 24379392 | tf_op jit(solution)/shard_map/dot_general | solution.py:55
  279.7 32.7 %reduce-scatter.2.cloned.1.call-done = bf16[640,512]{1,0:T(8,128)(2,1)} async-done(((bf16[640,2048]{1,0:T(8,128)(2,1)}), bf16[640,512]{1,0:T(8,128)(2,1)}) %reduce-scatter.2.cloned.1.call-update) | async-done | bytes 655376 | tf_op jit(solution)/shard_map/reduce_scatter | solution.py:254
  312.4 1.4 fusion.11
  313.8 6.6 %psum.23 = f32[640]{0:T(1024)S(1)} all-reduce(f32[640]{0:T(1024)S(1)} %fusion.11), channel_id=1, replica_groups=mesh['dp'=32,'mp'=4] {'mp'}, use_global_device_ids=true, to_apply=%region_23.24 | all-reduce | flops 640 | bytes 5120 | tf_op jit(solution)/shard_map/psum | solution.py:258
  320.4 1.6 fusion.10
  322.3 0.5 fusion
  322.8 1.4 reduce.20
  324.3 1.6 reshape.571
  325.9 9.7 %all-to-all-start.8 = ((bf16[32,2,8192]{2,1,0:T(2,128)(2,1)}), bf16[32,2,8192]{2,1,0:T(2,128)(2,1)}, u32[]{:S(2)}, u32[]{:S(2)}) async-start(bf16[32,2,8192]{2,1,0:T(2,128)(2,1)} %reshape.571), calls=%async_computation.9 | async-start | bytes 2097152 | tf_op jit(solution)/shard_map/all_to_all | solution.py:268
  335.5 0.5 log_subtract_fusion
  336.1 16.4 %all-to-all-done.8 = bf16[32,2,8192]{2,1,0:T(2,128)(2,1)} async-done(((bf16[32,2,8192]{2,1,0:T(2,128)(2,1)}), bf16[32,2,8192]{2,1,0:T(2,128)(2,1)}, u32[]{:S(2)}, u32[]{:S(2)}) %all-to-all-start.8) | async-done | bytes 1048608 | tf_op jit(solution)/shard_map/all_to_all | solution.py:268
  352.5 4.3 %reshape.572 = bf16[32,1,16384]{2,1,0:T(2,128)(2,1)S(1)} reshape(bf16[32,2,8192]{2,1,0:T(2,128)(2,1)} %all-to-all-done.8) | data formatting | bytes 2097152
  356.8 2.5 convolution_convert_fusion
  359.3 2.3 reshape.549
  (110 shorter events, 7.8 us)
Async XLA Ops:
  7.2 40.6 %copy-start.3 = (s32[1024]{0:T(1024)S(1)}, s32[1024]{0:T(1024)}, u32[]{:S(2)}) copy-start(s32[1024]{0:T(1024)} %param.10) | copy-start | bytes 12292
  29.0 14.5 %all-to-all-start = ((bf16[32,1,1]{2,1,0:T(2,128)(2,1)}), bf16[32,1,1]{2,1,0:T(2,128)(2,1)S(1)}, u32[]{:S(2)}, u32[]{:S(2)}) async-start(bf16[32,1,1]{2,1,0:T(2,128)(2,1)} %copy.74), calls=%async_computation | async-start | bytes 32768 | tf_op jit(solution)/shard_map/all_to_all | solution.py:128
  43.5 21.2 %all-to-all-start.1 = ((bf16[32,1,32,512]{3,2,1,0:T(8,128)(2,1)}), bf16[32,1,32,512]{3,2,1,0:T(8,128)(2,1)S(1)}, u32[]{:S(2)}, u32[]{:S(2)}) async-start(bf16[32,1,32,512]{3,2,1,0:T(8,128)(2,1)} %bitcast.5), calls=%async_computation.1 | async-start | bytes 2097152 | tf_op jit(solution)/shard_map/all_to_all | solution.py:126
  64.7 10.9 %all-to-all-start.2 = ((bf16[32,1,32]{2,1,0:T(2,128)(2,1)}), bf16[32,1,32]{2,1,0:T(2,128)(2,1)S(1)}, u32[]{:S(2)}, u32[]{:S(2)}) async-start(bf16[32,1,32]{2,1,0:T(2,128)(2,1)} %copy.77), calls=%async_computation.2 | async-start | bytes 32768 | tf_op jit(solution)/shard_map/all_to_all | solution.py:127
  71.6 10.6 %copy-start.5 = (s32[2]{0:T(128)S(1)}, s32[2]{0:T(128)}, u32[]{:S(2)}) copy-start(s32[2]{0:T(128)} %param.11) | copy-start | bytes 28
  71.6 11.4 %copy-start.4 = (s32[128]{0:T(128)S(1)}, s32[128]{0:T(128)}, u32[]{:S(2)}) copy-start(s32[128]{0:T(128)} %param.12) | copy-start | bytes 1540
  77.3 36.0 %copy-start.2 = (f32[2048]{0:T(1024)S(1)}, f32[2048]{0:T(1024)}, u32[]{:S(2)}) copy-start(f32[2048]{0:T(1024)} %param.14) | copy-start | bytes 24580
  77.3 35.4 %all-to-all-start.3 = ((bf16[4,640,512]{1,2,0:T(8,128)(2,1)}), bf16[4,640,512]{1,2,0:T(8,128)(2,1)S(1)}, u32[]{:S(2)}, u32[]{:S(2)}) async-start(bf16[4,640,512]{1,2,0:T(8,128)(2,1)} %broadcast_in_dim.21), calls=%async_computation.3 | async-start | bytes 5242880 | tf_op jit(solution)/shard_map/all_to_all | solution.py:17
  113.3 9.3 %slice-start.2 = ((s8[7340032]{0:T(1024)(128)(4,1)}), s8[4194304]{0:T(1024)(128)(4,1)S(1)}, s32[]{:S(2)}) async-start(s8[7340032]{0:T(1024)(128)(4,1)} %bitcast.104), calls=%async_computation.13 | async-start | bytes 8388608
  113.3 14.8 %slice-start = ((s8[7340032]{0:T(1024)(128)(4,1)}), s8[4194304]{0:T(1024)(128)(4,1)S(1)}, s32[]{:S(2)}) async-start(s8[7340032]{0:T(1024)(128)(4,1)} %bitcast.102), calls=%async_computation.11 | async-start | bytes 8388608
  114.0 8.7 %slice-start.3 = ((s8[7340032]{0:T(1024)(128)(4,1)}), s8[3145728]{0:T(1024)(128)(4,1)S(1)}, s32[]{:S(2)}) async-start(s8[7340032]{0:T(1024)(128)(4,1)} %bitcast.104), calls=%async_computation.14 | async-start | bytes 6291456
  114.0 14.2 %slice-start.1 = ((s8[7340032]{0:T(1024)(128)(4,1)}), s8[3145728]{0:T(1024)(128)(4,1)S(1)}, s32[]{:S(2)}) async-start(s8[7340032]{0:T(1024)(128)(4,1)} %bitcast.102), calls=%async_computation.12 | async-start | bytes 6291456
  122.7 5.5 %copy-start.7 = (f32[640,1792]{1,0:T(8,128)}, f32[640,1792]{1,0:T(8,128)S(1)}, u32[]{:S(2)}) copy-start(f32[640,1792]{1,0:T(8,128)S(1)} %fusion.87) | copy-start | bytes 13762564
  128.2 5.0 %copy-start.6 = (f32[640,1792]{1,0:T(8,128)}, f32[640,1792]{1,0:T(8,128)S(1)}, u32[]{:S(2)}) copy-start(f32[640,1792]{1,0:T(8,128)S(1)} %fusion.86) | copy-start | bytes 13762564
  133.2 5.0 %copy-start = (f32[3,8,32,512]{3,2,1,0:T(8,128)S(1)}, f32[3,8,32,512]{3,2,1,0:T(8,128)}, u32[]{:S(2)}) copy-start(f32[3,8,32,512]{3,2,1,0:T(8,128)} %copy.93) | copy-start | bytes 4718596
  133.2 18.1 %copy-start.1 = (bf16[128,512]{1,0:T(8,128)(2,1)S(1)}, bf16[128,512]{1,0:T(8,128)(2,1)}, u32[]{:S(2)}) copy-start(bf16[128,512]{1,0:T(8,128)(2,1)} %param.13) | copy-start | bytes 393220
  134.9 7.9 %all-to-all-start.4 = ((bf16[4,20,512]{2,1,0:T(8,128)(2,1)}), bf16[4,20,512]{2,1,0:T(8,128)(2,1)S(1)}, u32[]{:S(2)}, u32[]{:S(2)}) async-start(bf16[4,20,512]{2,1,0:T(8,128)(2,1)} %copy.79), calls=%async_computation.4 | async-start | bytes 196608 | tf_op jit(solution)/shard_map/all_to_all | solution.py:38
  144.8 13.9 %all-to-all-start.5 = ((bf16[32,2,256]{2,1,0:T(2,128)(2,1)}), bf16[32,2,256]{2,1,0:T(2,128)(2,1)S(1)}, u32[]{:S(2)}, u32[]{:S(2)}) async-start(bf16[32,2,256]{2,1,0:T(2,128)(2,1)} %reshape.567), calls=%async_computation.5 | async-start | bytes 65536 | tf_op jit(solution)/shard_map/all_to_all | solution.py:159
  201.4 17.7 %all-to-all-start.6 = ((bf16[32,8,513]{2,1,0:T(8,128)(2,1)}), bf16[32,8,513]{2,1,0:T(8,128)(2,1)S(1)}, u32[]{:S(2)}, u32[]{:S(2)}) async-start(bf16[32,8,513]{2,1,0:T(8,128)(2,1)} %pad_maximum_fusion), calls=%async_computation.6 | async-start | bytes 655360 | tf_op jit(solution)/shard_map/all_to_all | solution.py:38
  221.0 10.9 %all-to-all-start.7 = ((bf16[32,2,256]{2,1,0:T(2,128)(2,1)}), bf16[32,2,256]{2,1,0:T(2,128)(2,1)S(1)}, u32[]{:S(2)}, u32[]{:S(2)}) async-start(bf16[32,2,256]{2,1,0:T(2,128)(2,1)} %reshape.569), calls=%async_computation.7 | async-start | bytes 65536 | tf_op jit(solution)/shard_map/all_to_all | solution.py:228
  224.6 87.8 %reduce-scatter.2.cloned.1.call-start = ((), (), s32[]{:S(2)}) async-start(), calls=%async_computation.10 | async-start | bytes 3276800 | tf_op jit(solution)/shard_map/reduce_scatter | solution.py:254
  241.1 10.6 %slice-start.4 = ((s8[7340032]{0:T(1024)(128)(4,1)}), s8[4194304]{0:T(1024)(128)(4,1)S(1)}, s32[]{:S(2)}) async-start(s8[7340032]{0:T(1024)(128)(4,1)} %bitcast.106), calls=%async_computation.15 | async-start | bytes 8388608
  241.5 10.2 %slice-start.5 = ((s8[7340032]{0:T(1024)(128)(4,1)}), s8[3145728]{0:T(1024)(128)(4,1)S(1)}, s32[]{:S(2)}) async-start(s8[7340032]{0:T(1024)(128)(4,1)} %bitcast.106), calls=%async_computation.16 | async-start | bytes 6291456
  325.9 26.6 %all-to-all-start.8 = ((bf16[32,2,8192]{2,1,0:T(2,128)(2,1)}), bf16[32,2,8192]{2,1,0:T(2,128)(2,1)}, u32[]{:S(2)}, u32[]{:S(2)}) async-start(bf16[32,2,8192]{2,1,0:T(2,128)(2,1)} %reshape.571), calls=%async_computation.9 | async-start | bytes 2097152 | tf_op jit(solution)/shard_map/all_to_all | solution.py:268
Sparse Core Ops, SparseCore 0:
  279.7 32.6 reduce-scatter.1
